TPU v7x, 32 devices: a whole 2x2x4 slice. The times are simulated.
32 devices in a mesh: day: 2 (over x), row: 16 (over z, y, core).
Axes of the slice: x: 2, y: 2, z: 4, core: 2. Of those that a mesh axis runs over, the one named last changes fastest.
Arguments:
- spectra: bfloat16 [4096, 2, 2, 4096], P(('day', 'row')), parts along dimension 0, may hold values from -110 to 110
- pair_channels: int32 [64, 128, 2], P('row'), may hold values from 0 to 2047, as said below
- pair_live: int32 [64, 128], P('row'), may hold values from 0 to 1, as said below
Outputs:
- correlations: float32 [128, 128, 512], P(('day', 'row')), parts along dimension 0
There are 2 independent parts, one for each index of `day`. A program takes and returns all parts, laid end to end along the dimension named above; an argument that names none is the same for every part. Nothing has to cross between parts.
Inputs may be any that keep to these rules, and one draw needn't show every extreme that they name: `pair_channels`: pair slots of device i of row are tiles i * 4 to (i + 1) * 4 - 1; their first channels are that device's own channels i * 128 to (i + 1) * 128 - 1, and their second channels lie within 128 channels of the first; distances of exactly 128 occur on both sides. `pair_live`: in each device's pair slots (tile by tile, pair by pair) the live slots come first and the padding after; every device has 128 live slots or more, and one device's slots are all live.
All inputs are finite; a program needn't handle non-finite values.
Results may differ from a plain program's by a relative error of at most 0.003.
Values may be sent and summed in bfloat16 or wider, within the bound.
A program may use at most 192 MiB of HBM per device.

v0:
```python
import math
import jax
import jax.numpy as jnp
from jax import lax
from jax.sharding import PartitionSpec as P

WIN = 2
FREQ = 4096
BAND = 64
LAGS = 512
HALO = 128


def padded(block, sides, width):
    for axis, dim in sides:
        count = lax.axis_size(axis)
        forward = [(i, i + 1) for i in range(count - 1)]
        backward = [(target, source) for source, target in forward]
        low = lax.ppermute(
            lax.slice_in_dim(block, block.shape[dim] - width, None, axis=dim), axis, forward
        )
        high = lax.ppermute(lax.slice_in_dim(block, 0, width, axis=dim), axis, backward)
        block = jnp.concatenate([low, block, high], axis=dim)
    return block


def build_table(bin_total, lag_total):
    bin_index = jnp.arange(bin_total, dtype=jnp.int32)[:, None]
    shifts = jnp.arange(lag_total, dtype=jnp.int32)[None, :] - lag_total // 2
    phase_int = jnp.mod(bin_index * shifts, 2 * bin_total)
    angle_rad = phase_int.astype(jnp.float32) * (math.pi / bin_total)
    return jnp.concatenate([jnp.cos(angle_rad), -jnp.sin(angle_rad)], axis=0).astype(jnp.bfloat16)


def whiten(raw_rows, common):
    removed = raw_rows.astype(jnp.float32) - common[None]
    magnitude = jnp.sqrt(removed[:, :, 0] ** 2 + removed[:, :, 1] ** 2)
    row_count, window_count, bin_count = magnitude.shape
    banded = magnitude.reshape(row_count, window_count, bin_count // BAND, BAND)
    band_level = jnp.mean(banded, axis=3, keepdims=True) + 1e-06
    scaled = (
        removed.reshape(row_count, window_count, 2, bin_count // BAND, BAND)
        / band_level[:, :, None]
    )
    return scaled.reshape(raw_rows.shape).astype(jnp.bfloat16)


def cross_rows(first_rows, second_rows):
    first_f32 = first_rows.astype(jnp.float32)
    second_f32 = second_rows.astype(jnp.float32)
    real_part = jnp.sum(
        first_f32[:, :, 0] * second_f32[:, :, 0] + first_f32[:, :, 1] * second_f32[:, :, 1], axis=1
    )
    imag_part = jnp.sum(
        first_f32[:, :, 1] * second_f32[:, :, 0] - first_f32[:, :, 0] * second_f32[:, :, 1], axis=1
    )
    return jnp.concatenate([real_part, imag_part], axis=1).astype(jnp.bfloat16)


def body(spectra, pair_channels, pair_live):
    own_rows = spectra.shape[0]
    channels = own_rows * lax.axis_size("row")
    first_row = lax.axis_index("row") * own_rows - HALO
    local_sum = jnp.sum(spectra, axis=0, dtype=jnp.float32)
    common = lax.psum(local_sum, "row") / channels
    raw_band = padded(spectra, (("row", 0),), HALO)
    band_rows = whiten(raw_band, common)
    lag_matrix = build_table(FREQ, LAGS)
    norm_factor = 1.0 / math.sqrt(FREQ * WIN)
    tile_count = pair_channels.shape[0]
    tile_pairs = pair_channels.shape[1]
    group_count = tile_count // 4
    group_rows = 4 * tile_pairs
    pair_index = (pair_channels - first_row).reshape(group_count, group_rows, 2)
    weights = pair_live.astype(jnp.float32).reshape(group_count, group_rows)

    def correlate(index_rows, weight_rows):
        products = cross_rows(band_rows[index_rows[:, 0]], band_rows[index_rows[:, 1]])
        summed = jnp.dot(products, lag_matrix, preferred_element_type=jnp.float32)
        return summed * norm_factor * weight_rows[:, None]

    def one_group(operands):
        index_rows, weight_rows = operands
        outcome = correlate(index_rows, weight_rows)
        return outcome

    result = lax.map(one_group, (pair_index, weights))
    return result.reshape(tile_count, tile_pairs, LAGS)


def solution(mesh):
    placed = (P(("day", "row"), None, None, None), P("row", None, None), P("row", None))
    return jax.shard_map(
        body, mesh=mesh, in_specs=placed, out_specs=P(("day", "row"), None, None), check_vma=False
    )
```

profile of v0, /device:TPU:8, one launch (start us, length us, event | category | flops | bytes accessed | tf_op | source)
XLA Modules:
  0.0 495.4 jit_solution(6996535282205614045)
XLA Ops:
  6.5 7.1 %copy.11 = bf16[128,2,2,4096]{3,0,2,1:T(8,128)(2,1)} copy(bf16[128,2,2,4096]{3,2,1,0:T(2,128)(2,1)} %param.3) | data formatting | bytes 8388608 | tf_op args[0]
  13.6 1.9 collective-permute-start
  15.6 4.5 collective-permute-start.1
  20.1 6.4 %convert_reduce_fusion = f32[2,2,4096]{2,1,0:T(2,128)} fusion(bf16[128,2,2,4096]{3,2,1,0:T(2,128)(2,1)} %param.3), kind=kLoop, calls=%fused_computation.27 | loop fusion | flops 4177920 | bytes 4259840 | tf_op jit(solution)/shard_map/reduce_sum | solution.py:64
  26.5 0.0 all-reduce.2.cloned.1.call-update
  26.6 35.2 %cosine_convert_fusion = (bf16[4096,512]{1,0:T(8,128)(2,1)}, bf16[4096,512]{1,0:T(8,128)(2,1)}) fusion(s32[512]{0:T(512)S(1)} %iota_add_fusion), kind=kLoop, calls=%fused_computation.24 | loop fusion | flops 35651584 | bytes 8390656 | tf_op jit(solution)/shard_map/convert
  61.8 84.3 %all-reduce.2.cloned.1.call-done = f32[2,2,4096]{2,1,0:T(2,128)} async-done(((f32[2,2,4096]{2,1,0:T(2,128)}), f32[2,2,4096]{2,1,0:T(2,128)}) %all-reduce.2.cloned.1.call-update) | async-done | bytes 65552 | tf_op jit(solution)/shard_map/psum | solution.py:65
  146.2 0.9 broadcast_multiply_fusion
  147.0 0.0 collective-permute-done
  147.0 0.0 collective-permute-done.1
  147.1 7.4 %convert_subtract_fusion = f32[384,2,2,4096]{3,0,2,1:T(8,128)S(1)} fusion(bf16[128,2,2,4096]{3,0,2,1:T(8,128)(2,1)} %collective-permute-done.1, bf16[128,2,2,4096]{3,0,2,1:T(8,128)(2,1)} %copy.11, bf16[128,2,2,4096]{3,0,2,1:T(8,128)(2,1)} %collective-permute-done, f32[2,2,4096]{2,1,0:T(2,128)S(1)} %broadcast_multiply_fusion), kind=kLoop, calls=%fused_computation.3 | loop fusion | flops 44040192 | bytes 37814272 | tf_op jit(solution)/shard_map/sub | solution.py:36
  154.5 6.7 %fusion.1 = f32[384,2,1,4096]{3,0,2,1:T(8,128)} fusion(f32[384,2,2,4096]{3,0,2,1:T(8,128)S(1)} %convert_subtract_fusion), kind=kLoop, calls=%fused_computation.8 | loop fusion | flops 9437184 | bytes 37748736 | tf_op jit(solution)/shard_map/sqrt | solution.py:37
  161.2 12.6 %copy.14 = f32[384,2,1,4096]{0,3,1,2:T(8,128)} copy(f32[384,2,1,4096]{3,0,2,1:T(8,128)} %fusion.1) | data formatting | bytes 25165824 | tf_op jit(solution)/shard_map/sqrt | solution.py:37
  173.8 6.4 %reduce_sum.39 = f32[384,2,64]{0,2,1:T(8,128)S(1)} reduce(f32[384,2,64,64]{0,3,2,1:T(8,128)} %bitcast.9, f32[]{:T(128)} %constant.25.clone.1), dimensions={3}, to_apply=%region_2.0 | reduce | flops 3096576 | bytes 12779524 | tf_op jit(solution)/shard_map/reduce_sum | solution.py:40
  180.3 5.3 %div.29 = f32[384,2,64,64]{0,3,2,1:T(8,128)} broadcast(f32[384,2,64]{0,2,1:T(8,128)S(1)} %multiply_add_fusion), dimensions={0,1,2} | broadcast | bytes 12779520 | tf_op jit(solution)/shard_map/div | solution.py:42
  185.5 12.6 %copy.15 = f32[384,2,4096]{2,0,1:T(8,128)} copy(f32[384,2,4096]{0,2,1:T(8,128)} %bitcast.10) | data formatting | bytes 25165824 | tf_op jit(solution)/shard_map/div | solution.py:42
  198.2 10.2 %divide_convert_fusion = bf16[384,2,2,4096]{3,0,2,1:T(8,128)(2,1)S(1)} fusion(f32[384,2,4096]{2,0,1:T(8,128)} %copy.15, f32[2,2,4096]{2,1,0:T(2,128)S(1)} %broadcast_multiply_fusion, bf16[128,2,2,4096]{3,0,2,1:T(8,128)(2,1)} %collective-permute-done.1, bf16[128,2,2,4096]{3,0,2,1:T(8,128)(2,1)} %copy.11, bf16[128,2,2,4096]{3,0,2,1:T(8,128)(2,1)} %collective-permute-done), kind=kLoop, calls=%fused_computation.2 | loop fusion | flops 56623104 | bytes 37814272 | tf_op jit(solution)/shard_map/convert_element_type | solution.py:45
  208.4 30.0 %copy.17 = bf16[384,2,2,4096]{3,2,1,0:T(2,128)(2,1)} copy(bf16[384,2,2,4096]{3,0,2,1:T(8,128)(2,1)S(1)} %divide_convert_fusion) | data formatting | bytes 25165824 | tf_op jit(solution)/shard_map/convert_element_type | solution.py:45
  238.3 47.0 %gather_fusion = bf16[512,2,2,4096]{3,2,1,0:T(2,128)(2,1)} fusion(bf16[384,2,2,4096]{3,2,1,0:T(2,128)(2,1)} %copy.17, s32[1024]{0:T(1024)S(1)} %pad_clamp_fusion.1), kind=kCustom, calls=%fused_computation | custom fusion | bytes 33556480 | tf_op jit(solution)/shard_map/while/body/eval_jaxpr/gather | solution.py:78
  285.4 17.6 %convert_element_type.33 = f32[512,2,2,4096]{3,2,1,0:T(2,128)} convert(bf16[512,2,2,4096]{3,2,1,0:T(2,128)(2,1)} %gather_fusion) | non-fusion elementwise | flops 8388608 | bytes 50331648 | tf_op jit(solution)/shard_map/while/body/eval_jaxpr/convert_element_type | solution.py:49
  303.0 46.8 %gather_fusion.1 = bf16[512,2,2,4096]{3,2,1,0:T(2,128)(2,1)} fusion(bf16[384,2,2,4096]{3,2,1,0:T(2,128)(2,1)} %copy.17, s32[1024]{0:T(1024)S(1)} %pad_clamp_fusion), kind=kCustom, calls=%fused_computation.1 | custom fusion | bytes 33556480 | tf_op jit(solution)/shard_map/while/body/eval_jaxpr/gather | solution.py:78
  349.8 17.6 %convert_element_type.34 = f32[512,2,2,4096]{3,2,1,0:T(2,128)} convert(bf16[512,2,2,4096]{3,2,1,0:T(2,128)(2,1)} %gather_fusion.1) | non-fusion elementwise | flops 8388608 | bytes 50331648 | tf_op jit(solution)/shard_map/while/body/eval_jaxpr/convert_element_type | solution.py:50
  367.4 113.5 %add_reduce_fusion = (bf16[512,4096]{1,0:T(8,128)(2,1)S(1)}, bf16[512,4096]{1,0:T(8,128)(2,1)S(1)}) fusion(f32[512,2,2,4096]{3,2,1,0:T(2,128)} %convert_element_type.34, f32[512,2,2,4096]{3,2,1,0:T(2,128)} %convert_element_type.33), kind=kLoop, calls=%fused_computation.5 | loop fusion | flops 29360128 | bytes 75497472 | tf_op jit(solution)/shard_map/while/body/eval_jaxpr/reduce_sum | solution.py:51
  480.9 7.6 %fusion.15 = f32[512,512]{1,0:T(8,128)} fusion(bf16[4096,512]{1,0:T(8,128)(2,1)} %get-tuple-element.28, bf16[4096,512]{1,0:T(8,128)(2,1)S(1)} %copy-done, bf16[512,4096]{1,0:T(8,128)(2,1)S(1)} %get-tuple-element.16, bf16[512,4096]{1,0:T(8,128)(2,1)S(1)} %get-tuple-element.15, f32[512]{0:T(512)S(1)} %multiply_bitcast_fusion), kind=kOutput, calls=%fused_computation.29 | convolution fusion | flops 4328783872 | bytes 17827840 | tf_op jit(solution)/shard_map/while/body/eval_jaxpr/dot_general | solution.py:79
  (14 shorter events, 0.1 us)
Async XLA Ops:
  6.5 20.0 %copy-start.1 = (s32[4,128,2]{1,2,0:T(2,128)S(1)}, s32[4,128,2]{1,2,0:T(2,128)}, u32[]{:S(2)}) copy-start(s32[4,128,2]{1,2,0:T(2,128)} %param.4) | copy-start | bytes 12292
  6.5 20.0 %copy-start.2 = (s32[4,128]{1,0:T(4,128)S(1)}, s32[4,128]{1,0:T(4,128)}, u32[]{:S(2)}) copy-start(s32[4,128]{1,0:T(4,128)} %param.5) | copy-start | bytes 6148
  6.5 139.6 %all-reduce.2.cloned.1.call-start = ((), (), s32[]{:S(2)}) async-start(), calls=%async_computation | async-start | bytes 131072 | tf_op jit(solution)/shard_map/psum | solution.py:65
  13.6 133.4 %collective-permute-start = (bf16[128,2,2,4096]{3,0,2,1:T(8,128)(2,1)}, bf16[128,2,2,4096]{3,0,2,1:T(8,128)(2,1)}, u32[]{:S(2)}, u32[]{:S(2)}) collective-permute-start(bf16[128,2,2,4096]{3,0,2,1:T(8,128)(2,1)} %copy.11), channel_id=1, source_target_pairs={{0,1},{1,2},{2,3},{3,4},{4,5},{5,6},{6,7},{7,8},{8,9},{9,10},{10,1... | collective-permute-start | bytes 12582920 | tf_op jit(solution)/shard_map/ppermute | solution.py:19
  15.6 131.5 %collective-permute-start.1 = (bf16[128,2,2,4096]{3,0,2,1:T(8,128)(2,1)}, bf16[128,2,2,4096]{3,0,2,1:T(8,128)(2,1)}, u32[]{:S(2)}, u32[]{:S(2)}) collective-permute-start(bf16[128,2,2,4096]{3,0,2,1:T(8,128)(2,1)} %copy.11), channel_id=1, source_target_pairs={{1,0},{2,1},{3,2},{4,3},{5,4},{6,5},{7,6},{8,7},{9,8},{10,9},{11,1... | collective-permute-start | bytes 12582920 | tf_op jit(solution)/shard_map/ppermute | solution.py:22
  367.4 113.5 %copy-start = (bf16[4096,512]{1,0:T(8,128)(2,1)S(1)}, bf16[4096,512]{1,0:T(8,128)(2,1)}, u32[]{:S(2)}) copy-start(bf16[4096,512]{1,0:T(8,128)(2,1)} %get-tuple-element.26) | copy-start | bytes 12582916
Sparse Core Ops, SparseCore 0:
  26.6 119.4 all-reduce.1
where the time goes:
time: 497 us; the launch traced here: 495 us
  other arithmetic  222 us (45%)
  local copies, waits for them, and re-layouts  161 us (32%)
  waiting for transfers between devices  84.4 us (17%)
  between operations  13.5 us (3%)
  matrix products  7.65 us (2%)
  starting transfers between devices  6.45 us (1%)
    reduce_sum x1, other arithmetic, cross_rows(): jnp.sum(first_f32[:, :, 0] * second_f32[:, :, 0] + first_f32[:, :, 1] * s...  114 us
    psum x1, waiting for transfers between devices, body(): common = lax.psum(local_sum, 'row') / channels  84.3 us
    gather x1, local copies, waits for them, and re-layouts, correlate(): band_rows[index_rows[:, 0]]  47 us
    gather x1, local copies, waits for them, and re-layouts, correlate(): band_rows[index_rows[:, 1]]  46.8 us
    another operation x1, other arithmetic  35.2 us
    convert_element_type x1, local copies, waits for them, and re-layouts, whiten(): return scaled.reshape(raw_rows.shape).astype(jnp.bfloat16)  30 us
    div x2, local copies, waits for them, and re-layouts, whiten(): removed.reshape(row_count, window_count, 2, bin_count // BAND, BAND)  17.9 us
    convert_element_type x1, other arithmetic, cross_rows(): first_f32 = first_rows.astype(jnp.float32)  17.6 us
  transfers between devices with their start and end apart: 3, of which 1 were waited for; matrix products, arithmetic and copies ran while one was open for 9% of the time, Pallas kernels for 0%

commit v1 on v0

--- a/solution.py
+++ b/solution.py
@@ -62,7 +62,7 @@
     channels = own_rows * lax.axis_size("row")
     first_row = lax.axis_index("row") * own_rows - HALO
     local_sum = jnp.sum(spectra, axis=0, dtype=jnp.float32)
-    common = lax.psum(local_sum, "row") / channels
+    common = jnp.sum(lax.all_gather(local_sum, "row"), axis=0) / channels
     raw_band = padded(spectra, (("row", 0),), HALO)
     band_rows = whiten(raw_band, common)
     lag_matrix = build_table(FREQ, LAGS)

time: 497 us -> 463 us (0.932)
  the two profiles are of different devices: /device:TPU:8 before, /device:TPU:25 now
where the time goes in v1:
time: 463 us; the launch traced here: 461 us
  other arithmetic  223 us (48%)
  local copies, waits for them, and re-layouts  161 us (35%)
  waiting for transfers between devices  50.5 us (11%)
  between operations  13.5 us (3%)
  matrix products  7.64 us (2%)
  starting transfers between devices  5.62 us (1%)
    reduce_sum x1, other arithmetic, cross_rows(): jnp.sum(first_f32[:, :, 0] * second_f32[:, :, 0] + first_f32[:, :, 1] * s...  114 us
    gather x1, local copies, waits for them, and re-layouts, correlate(): band_rows[index_rows[:, 0]]  47 us
    gather x1, local copies, waits for them, and re-layouts, correlate(): band_rows[index_rows[:, 1]]  46.8 us
    another operation x1, other arithmetic  35.2 us
    ppermute x1, waiting for transfers between devices, padded(): lax.ppermute(lax.slice_in_dim(block, 0, width, axis=dim), axis, backward)  32.6 us
    convert_element_type x1, local copies, waits for them, and re-layouts, whiten(): return scaled.reshape(raw_rows.shape).astype(jnp.bfloat16)  30 us
    div x2, local copies, waits for them, and re-layouts, whiten(): removed.reshape(row_count, window_count, 2, bin_count // BAND, BAND)  17.9 us
    all_gather x1, waiting for transfers between devices, body(): common = jnp.sum(lax.all_gather(local_sum, 'row'), axis=0) / channels  17.8 us
  transfers between devices with their start and end apart: 3, of which 2 were waited for; matrix products, arithmetic and copies ran while one was open for 9% of the time, Pallas kernels for 0%

profile of v1, /device:TPU:25, one launch (start us, length us, event | category | flops | bytes accessed | tf_op | source)
XLA Modules:
  0.0 461.4 jit_solution(1477528875200243284)
XLA Ops:
  6.5 7.1 %copy.14 = bf16[128,2,2,4096]{3,0,2,1:T(8,128)(2,1)} copy(bf16[128,2,2,4096]{3,2,1,0:T(2,128)(2,1)} %param.3) | data formatting | bytes 8388608 | tf_op args[0]
  13.6 3.7 collective-permute-start
  17.3 1.9 collective-permute-start.1
  19.3 6.4 %convert_reduce_fusion = f32[2,2,4096]{2,1,0:T(2,128)} fusion(bf16[128,2,2,4096]{3,2,1,0:T(2,128)(2,1)} %param.3), kind=kLoop, calls=%fused_computation.27 | loop fusion | flops 4177920 | bytes 4259840 | tf_op jit(solution)/shard_map/reduce_sum | solution.py:64
  25.6 0.0 all-gather.3.cloned.1.call-update
  25.8 35.2 %cosine_convert_fusion = (bf16[4096,512]{1,0:T(8,128)(2,1)}, bf16[4096,512]{1,0:T(8,128)(2,1)}) fusion(s32[512]{0:T(512)S(1)} %iota_add_fusion), kind=kLoop, calls=%fused_computation.24 | loop fusion | flops 35651584 | bytes 8390656 | tf_op jit(solution)/shard_map/convert
  61.0 17.8 %all-gather.3.cloned.1.call-done = f32[32,2,4096]{2,1,0:T(2,128)} async-done(((f32[2,2,4096]{2,1,0:T(2,128)}), f32[32,2,4096]{2,1,0:T(2,128)}) %all-gather.3.cloned.1.call-update) | async-done | bytes 1048592 | tf_op jit(solution)/shard_map/all_gather | solution.py:65
  78.8 1.6 reduce_sum.48
  80.5 0.0 collective-permute-done
  80.5 32.6 %collective-permute-done.1 = bf16[128,2,2,4096]{3,0,2,1:T(8,128)(2,1)} collective-permute-done((bf16[128,2,2,4096]{3,0,2,1:T(8,128)(2,1)}, bf16[128,2,2,4096]{3,0,2,1:T(8,128)(2,1)}, u32[]{:S(2)}, u32[]{:S(2)}) %collective-permute-start.1) | collective-permute-done | bytes 4194336 | tf_op jit(solution)/shard_map/ppermute | solution.py:22
  113.1 7.4 %convert_subtract_fusion = f32[384,2,2,4096]{3,0,2,1:T(8,128)S(1)} fusion(bf16[128,2,2,4096]{3,0,2,1:T(8,128)(2,1)} %collective-permute-done.1, bf16[128,2,2,4096]{3,0,2,1:T(8,128)(2,1)} %copy.14, bf16[128,2,2,4096]{3,0,2,1:T(8,128)(2,1)} %collective-permute-done, f32[2,2,4096]{2,1,0:T(2,128)S(1)} %broadcast_multiply_fusion), kind=kLoop, calls=%fused_computation.3 | loop fusion | flops 44040192 | bytes 37814272 | tf_op jit(solution)/shard_map/sub | solution.py:36
  120.5 6.7 %fusion.1 = f32[384,2,1,4096]{3,0,2,1:T(8,128)} fusion(f32[384,2,2,4096]{3,0,2,1:T(8,128)S(1)} %convert_subtract_fusion), kind=kLoop, calls=%fused_computation.8 | loop fusion | flops 9437184 | bytes 37748736 | tf_op jit(solution)/shard_map/sqrt | solution.py:37
  127.2 12.6 %copy.17 = f32[384,2,1,4096]{0,3,1,2:T(8,128)} copy(f32[384,2,1,4096]{3,0,2,1:T(8,128)} %fusion.1) | data formatting | bytes 25165824 | tf_op jit(solution)/shard_map/sqrt | solution.py:37
  139.8 6.4 %reduce_sum.49 = f32[384,2,64]{0,2,1:T(8,128)S(1)} reduce(f32[384,2,64,64]{0,3,2,1:T(8,128)} %bitcast.10, f32[]{:T(128)} %constant.25.clone.1), dimensions={3}, to_apply=%region_2.0 | reduce | flops 3096576 | bytes 12779524 | tf_op jit(solution)/shard_map/reduce_sum | solution.py:40
  146.3 5.3 %div.29 = f32[384,2,64,64]{0,3,2,1:T(8,128)} broadcast(f32[384,2,64]{0,2,1:T(8,128)S(1)} %multiply_add_fusion), dimensions={0,1,2} | broadcast | bytes 12779520 | tf_op jit(solution)/shard_map/div | solution.py:42
  151.6 12.6 %copy.18 = f32[384,2,4096]{2,0,1:T(8,128)} copy(f32[384,2,4096]{0,2,1:T(8,128)} %bitcast.11) | data formatting | bytes 25165824 | tf_op jit(solution)/shard_map/div | solution.py:42
  164.2 10.2 %divide_convert_fusion = bf16[384,2,2,4096]{3,0,2,1:T(8,128)(2,1)S(1)} fusion(f32[384,2,4096]{2,0,1:T(8,128)} %copy.18, f32[2,2,4096]{2,1,0:T(2,128)S(1)} %broadcast_multiply_fusion, bf16[128,2,2,4096]{3,0,2,1:T(8,128)(2,1)} %collective-permute-done.1, bf16[128,2,2,4096]{3,0,2,1:T(8,128)(2,1)} %copy.14, bf16[128,2,2,4096]{3,0,2,1:T(8,128)(2,1)} %collective-permute-done), kind=kLoop, calls=%fused_computation.2 | loop fusion | flops 56623104 | bytes 37814272 | tf_op jit(solution)/shard_map/convert_element_type | solution.py:45
  174.4 30.0 %copy.20 = bf16[384,2,2,4096]{3,2,1,0:T(2,128)(2,1)} copy(bf16[384,2,2,4096]{3,0,2,1:T(8,128)(2,1)S(1)} %divide_convert_fusion) | data formatting | bytes 25165824 | tf_op jit(solution)/shard_map/convert_element_type | solution.py:45
  204.3 47.0 %gather_fusion = bf16[512,2,2,4096]{3,2,1,0:T(2,128)(2,1)} fusion(bf16[384,2,2,4096]{3,2,1,0:T(2,128)(2,1)} %copy.20, s32[1024]{0:T(1024)S(1)} %pad_clamp_fusion.1), kind=kCustom, calls=%fused_computation | custom fusion | bytes 33556480 | tf_op jit(solution)/shard_map/while/body/eval_jaxpr/gather | solution.py:78
  251.4 17.6 %convert_element_type.33 = f32[512,2,2,4096]{3,2,1,0:T(2,128)} convert(bf16[512,2,2,4096]{3,2,1,0:T(2,128)(2,1)} %gather_fusion) | non-fusion elementwise | flops 8388608 | bytes 50331648 | tf_op jit(solution)/shard_map/while/body/eval_jaxpr/convert_element_type | solution.py:49
  269.0 46.8 %gather_fusion.1 = bf16[512,2,2,4096]{3,2,1,0:T(2,128)(2,1)} fusion(bf16[384,2,2,4096]{3,2,1,0:T(2,128)(2,1)} %copy.20, s32[1024]{0:T(1024)S(1)} %pad_clamp_fusion), kind=kCustom, calls=%fused_computation.1 | custom fusion | bytes 33556480 | tf_op jit(solution)/shard_map/while/body/eval_jaxpr/gather | solution.py:78
  315.8 17.6 %convert_element_type.34 = f32[512,2,2,4096]{3,2,1,0:T(2,128)} convert(bf16[512,2,2,4096]{3,2,1,0:T(2,128)(2,1)} %gather_fusion.1) | non-fusion elementwise | flops 8388608 | bytes 50331648 | tf_op jit(solution)/shard_map/while/body/eval_jaxpr/convert_element_type | solution.py:50
  333.4 113.5 %add_reduce_fusion = (bf16[512,4096]{1,0:T(8,128)(2,1)S(1)}, bf16[512,4096]{1,0:T(8,128)(2,1)S(1)}) fusion(f32[512,2,2,4096]{3,2,1,0:T(2,128)} %convert_element_type.34, f32[512,2,2,4096]{3,2,1,0:T(2,128)} %convert_element_type.33), kind=kLoop, calls=%fused_computation.5 | loop fusion | flops 29360128 | bytes 75497472 | tf_op jit(solution)/shard_map/while/body/eval_jaxpr/reduce_sum | solution.py:51
  446.9 7.6 %fusion.15 = f32[512,512]{1,0:T(8,128)} fusion(bf16[4096,512]{1,0:T(8,128)(2,1)} %get-tuple-element.28, bf16[4096,512]{1,0:T(8,128)(2,1)S(1)} %copy-done, bf16[512,4096]{1,0:T(8,128)(2,1)S(1)} %get-tuple-element.16, bf16[512,4096]{1,0:T(8,128)(2,1)S(1)} %get-tuple-element.15, f32[512]{0:T(512)S(1)} %multiply_bitcast_fusion), kind=kOutput, calls=%fused_computation.29 | convolution fusion | flops 4328783872 | bytes 17827840 | tf_op jit(solution)/shard_map/while/body/eval_jaxpr/dot_general | solution.py:79
  (15 shorter events, 0.1 us)
Async XLA Ops:
  6.5 19.1 %copy-start.1 = (s32[4,128,2]{1,2,0:T(2,128)S(1)}, s32[4,128,2]{1,2,0:T(2,128)}, u32[]{:S(2)}) copy-start(s32[4,128,2]{1,2,0:T(2,128)} %param.4) | copy-start | bytes 12292
  6.5 19.2 %copy-start.2 = (s32[4,128]{1,0:T(4,128)S(1)}, s32[4,128]{1,0:T(4,128)}, u32[]{:S(2)}) copy-start(s32[4,128]{1,0:T(4,128)} %param.5) | copy-start | bytes 6148
  6.5 72.3 %all-gather.3.cloned.1.call-start = ((), (), s32[]{:S(2)}) async-start(), calls=%async_computation | async-start | bytes 1114112 | tf_op jit(solution)/shard_map/all_gather | solution.py:65
  13.6 66.9 %collective-permute-start = (bf16[128,2,2,4096]{3,0,2,1:T(8,128)(2,1)}, bf16[128,2,2,4096]{3,0,2,1:T(8,128)(2,1)}, u32[]{:S(2)}, u32[]{:S(2)}) collective-permute-start(bf16[128,2,2,4096]{3,0,2,1:T(8,128)(2,1)} %copy.14), channel_id=1, source_target_pairs={{0,1},{1,2},{2,3},{3,4},{4,5},{5,6},{6,7},{7,8},{8,9},{9,10},{10,1... | collective-permute-start | bytes 12582920 | tf_op jit(solution)/shard_map/ppermute | solution.py:19
  17.3 95.8 %collective-permute-start.1 = (bf16[128,2,2,4096]{3,0,2,1:T(8,128)(2,1)}, bf16[128,2,2,4096]{3,0,2,1:T(8,128)(2,1)}, u32[]{:S(2)}, u32[]{:S(2)}) collective-permute-start(bf16[128,2,2,4096]{3,0,2,1:T(8,128)(2,1)} %copy.14), channel_id=1, source_target_pairs={{1,0},{2,1},{3,2},{4,3},{5,4},{6,5},{7,6},{8,7},{9,8},{10,9},{11,1... | collective-permute-start | bytes 12582920 | tf_op jit(solution)/shard_map/ppermute | solution.py:22
  333.4 113.5 %copy-start = (bf16[4096,512]{1,0:T(8,128)(2,1)S(1)}, bf16[4096,512]{1,0:T(8,128)(2,1)}, u32[]{:S(2)}) copy-start(bf16[4096,512]{1,0:T(8,128)(2,1)} %get-tuple-element.26) | copy-start | bytes 12582916
Sparse Core Ops, SparseCore 0:
  25.8 53.0 all-gather.2
